TPU v7x, 128 devices: a whole 4x4x4 slice. The times are simulated.
128 devices in a mesh: gx: 8 (over z_lo, y), gy: 16 (over z_hi, x, core).
Axes of the slice: x: 4, y: 4, z: 4 (z_hi: 2, z_lo: 2; z = z_hi * 2 + z_lo), core: 2. Of those that a mesh axis runs over, the one named last changes fastest.
Arguments:
- ice_displacement: float32 [2, 64, 128, 128], P(None, 'gx', 'gy'), may hold values from -1.8 to 1.8
- ice_velocity: float32 [2, 64, 128, 128], P(None, 'gx', 'gy'), may hold values from -6 to 6
- jitter: float32 [2, 64, 128, 128], P(None, 'gx', 'gy'), may hold values from -0.2 to 0.2
- bond_mask: int32 [64, 128, 9], P('gx', 'gy'), may hold values from -2147483648 to 2147483647, as said below
- contact_node: int32 [128, 128], P('gy'), may hold values from 0 to 8388607, as said below
- intersection: float32 [128, 128], P('gy'), may hold values from -0.5 to 1
- shell_deflection: float32 [1024, 8192], P('gx', 'gy'), may hold values from -1.8 to 1.8
- shell_velocity: float32 [1024, 8192], P('gx', 'gy'), may hold values from -6 to 6
Outputs:
- ice_moved: float32 [2, 64, 128, 128], P(None, 'gx', 'gy')
- ice_speed: float32 [2, 64, 128, 128], P(None, 'gx', 'gy')
- shell_moved: float32 [1024, 8192], P('gx', 'gy')
- shell_speed: float32 [1024, 8192], P('gx', 'gy')
Inputs may be any that keep to these rules, and one draw needn't show every extreme that they name: Bit 4 * i + k of bond_mask[a, b, s] (bit 31 being the sign bit) is 1 where the bonds from the points of lengthwise row i of tile (a, b) to the points q with 4 q // 128 == k of neighbouring tile s are intact. contact_node = r * 8192 + c for shell row r and column c; for point q of tile column t, c // 4 == t * 16 + q % 16 and r // 128 == q // 16.
All inputs are finite; a program needn't handle non-finite values.
Results may differ from a plain program's by a relative error of at most 0.0001.
Values sent between devices are 32-bit elements; how exact they have to be, the bound alone decides.
A program may use at most 64 MiB of HBM per device.

v0:
```python
import jax
import jax.numpy as jnp
from jax import lax
from jax.sharding import PartitionSpec as P

TILE_X = 8
TILE_Y = 16
PTS = 128
STEPS = 2
BOND_C = 1.0
HORIZON = 3.5
DELTA_SQ = 0.25
PENALTY = 4.0
BEND = 0.5
STEP_DT = 0.2


def extended(cells, sides, width):
    for axis, dim in sides:
        count = lax.axis_size(axis)
        ends = count - 1
        head = lax.slice_in_dim(cells, 0, width, axis=dim)
        tail = lax.slice_in_dim(cells, cells.shape[dim] - width, cells.shape[dim], axis=dim)
        cells = jnp.concatenate(
            [
                lax.ppermute(tail, axis, [(i, (i + 1) % count) for i in range(ends)]),
                cells,
                lax.ppermute(head, axis, [((i + 1) % count, i) for i in range(ends)]),
            ],
            axis=dim,
        )
    return cells


def spread(array, axis, root):
    mine = lax.axis_index(axis) == root
    return lax.psum(jnp.where(mine, array, jnp.zeros_like(array)), axis)


def pair_force(center, nearby, words, shift_x, shift_y):
    points = jnp.arange(TILE_X * TILE_Y, dtype=jnp.int32)
    bit_index = 4 * (points // TILE_Y)[:, None] + (4 * points // PTS)[None, :]
    intact = jnp.right_shift(words[..., None, None], bit_index) & 1
    lengthwise = (points // TILE_Y).astype(jnp.float32)
    sideways = (points % TILE_Y).astype(jnp.float32)
    base_x = shift_x * TILE_X + lengthwise[None, :] - lengthwise[:, None]
    base_y = shift_y * TILE_Y + sideways[None, :] - sideways[:, None]
    rest_x = base_x + (nearby[2][..., None, :] - center[2][..., :, None])
    rest_y = base_y + (nearby[3][..., None, :] - center[3][..., :, None])
    now_x = rest_x + (nearby[0][..., None, :] - center[0][..., :, None])
    now_y = rest_y + (nearby[1][..., None, :] - center[1][..., :, None])
    radius = jnp.sqrt(rest_x * rest_x + rest_y * rest_y + DELTA_SQ)
    stretched = jnp.sqrt(now_x * now_x + now_y * now_y + DELTA_SQ)
    reach = jnp.maximum(1.0 - radius / HORIZON, 0.0)
    factor = (
        BOND_C
        * intact.astype(jnp.float32)
        * reach
        * reach
        * (stretched - radius)
        / (radius * stretched)
    )
    return jnp.stack([jnp.sum(factor * now_x, axis=-1), jnp.sum(factor * now_y, axis=-1)])


def ice_forces(displacement, jitter_padded, bond_mask):
    tiles_x = displacement.shape[1]
    tiles_y = displacement.shape[2]
    moved_padded = extended(displacement, (("gx", 1), ("gy", 2)), 1)
    padded = jnp.concatenate([moved_padded, jitter_padded], axis=0)
    row_ids = lax.axis_index("gx") * tiles_x + jnp.arange(-1, tiles_x + 1, dtype=jnp.int32)
    col_ids = lax.axis_index("gy") * tiles_y + jnp.arange(-1, tiles_y + 1, dtype=jnp.int32)
    rows_ok = ((row_ids >= 0) & (row_ids < tiles_x * lax.axis_size("gx"))).astype(jnp.float32)
    cols_ok = ((col_ids >= 0) & (col_ids < tiles_y * lax.axis_size("gy"))).astype(jnp.float32)
    present = rows_ok[:, None] * cols_ok[None, :]
    center = padded[:, 1 : 1 + tiles_x, 1 : 1 + tiles_y]
    totals = jnp.zeros((2, tiles_x, tiles_y, displacement.shape[3]), jnp.float32)
    for offset in range(9):
        shift_x = offset // 3 - 1
        shift_y = offset % 3 - 1
        nearby = padded[:, 1 + shift_x : 1 + shift_x + tiles_x, 1 + shift_y : 1 + shift_y + tiles_y]
        weight = present[1 + shift_x : 1 + shift_x + tiles_x, 1 + shift_y : 1 + shift_y + tiles_y]
        totals = (
            totals
            + pair_force(center, nearby, bond_mask[:, :, offset], shift_x, shift_y)
            * weight[None, :, :, None]
        )
    return totals


def laplace(field):
    return (
        field[2:, 1:-1]
        + field[:-2, 1:-1]
        + field[1:-1, 2:]
        + field[1:-1, :-2]
        - 4.0 * field[1:-1, 1:-1]
    )


def on_device(
    ice_displacement,
    ice_velocity,
    jitter,
    bond_mask,
    contact_node,
    intersection,
    shell_deflection,
    shell_velocity,
):
    shell_rows = shell_deflection.shape[0]
    shell_cols = shell_deflection.shape[1]
    node_count = shell_rows * shell_cols
    width_all = shell_cols * lax.axis_size("gy")
    row_of = contact_node // width_all
    col_of = contact_node % width_all
    owned = (row_of // shell_rows == lax.axis_index("gx")) & (
        col_of // shell_cols == lax.axis_index("gy")
    )
    local_ids = (row_of % shell_rows * shell_cols + col_of % shell_cols).reshape(-1)
    front_flag = (lax.axis_index("gx") == lax.axis_size("gx") - 1).astype(jnp.float32)
    jitter_padded = extended(jitter, (("gx", 1), ("gy", 2)), 1)
    for iteration in range(STEPS):
        forces = ice_forces(ice_displacement, jitter_padded, bond_mask)
        front_gap = ice_displacement[0, -1] + intersection
        gaps = spread(front_gap, "gx", lax.axis_size("gx") - 1)
        reached = shell_deflection.reshape(-1)[local_ids].reshape(gaps.shape)
        pushes = jnp.where(owned, PENALTY * jnp.maximum(gaps - reached, 0.0), 0.0)
        loading = jax.ops.segment_sum(pushes.reshape(-1), local_ids, num_segments=node_count)
        loading = loading.reshape(shell_rows, shell_cols)
        my_pushes = lax.psum(pushes, "gx") * front_flag
        forces = forces.at[0, -1].add(-my_pushes)
        shell_padded = extended(shell_deflection, (("gx", 0), ("gy", 1)), 2)
        bending = laplace(laplace(shell_padded))
        ice_velocity = ice_velocity + STEP_DT * forces
        ice_displacement = ice_displacement + STEP_DT * ice_velocity
        shell_velocity = shell_velocity + STEP_DT * (loading - BEND * bending)
        shell_deflection = shell_deflection + STEP_DT * shell_velocity
    return (ice_displacement, ice_velocity, shell_deflection, shell_velocity)


def solution(mesh):
    in_specs = (
        P(None, "gx", "gy", None),
        P(None, "gx", "gy", None),
        P(None, "gx", "gy", None),
        P("gx", "gy", None),
        P("gy", None),
        P("gy", None),
        P("gx", "gy"),
        P("gx", "gy"),
    )
    out_specs = (P(None, "gx", "gy", None), P(None, "gx", "gy", None), P("gx", "gy"), P("gx", "gy"))
    return jax.shard_map(
        on_device, mesh=mesh, in_specs=in_specs, out_specs=out_specs, check_vma=False
    )
```

profile of v0, /device:TPU:47, one launch (start us, length us, event | category | flops | bytes accessed | tf_op | source)
XLA Modules:
  0.0 394.4 jit_solution(1697325926070671556)
XLA Ops:
  19.4 15.6 %psum.28 = f32[8,128]{1,0:T(8,128)S(1)} all-reduce(f32[8,128]{1,0:T(8,128)S(1)} %fusion.96), channel_id=1, replica_groups=mesh['gx'=8,'gy'=16] {'gx'}, use_global_device_ids=true, to_apply=%region_19.20 | all-reduce | flops 1024 | bytes 8192 | tf_op jit(solution)/shard_map/psum | solution.py:37
  35.2 6.2 %gather_fusion = f32[1024]{0:T(1024)S(1)} fusion(f32[65536]{0:T(1024)S(1)} %bitcast.195, s32[1024]{0:T(1024)S(1)} %broadcast_clamp_fusion), kind=kCustom, calls=%fused_computation | custom fusion | bytes 12288 | tf_op jit(solution)/shard_map/gather | solution.py:127
  42.3 11.0 %multiply_reduce_fusion.27 = (f32[8,8,128]{2,1,0:T(8,128)S(1)}, f32[8,8,128]{2,1,0:T(8,128)S(1)}) fusion(f32[8,8,128]{2,1,0:T(8,128)S(1)} %get-tuple-element.167, f32[8,8,128]{2,1,0:T(8,128)S(1)} %get-tuple-element.165, f32[128,128]{1,0:T(8,128)S(1)} %get-tuple-element.200, f32[8,8,128]{2,1,0:T(8,128)S(1)} %get-tuple-element.166, ...), kind=kLoop, calls=%fused_computation.95 | loop fusion | flops 33538048 | bytes 393472 | tf_op jit(solution)/shard_map/reduce_sum | solution.py:63
  53.3 16.0 %psum.29 = f32[8,128]{1,0:T(8,128)S(1)} all-reduce(f32[8,128]{1,0:T(8,128)S(1)} %get-tuple-element.86), channel_id=1, replica_groups=mesh['gx'=8,'gy'=16] {'gx'}, use_global_device_ids=true, to_apply=%region_20.21 | all-reduce | flops 1024 | bytes 8192 | tf_op jit(solution)/shard_map/psum | solution.py:131
  69.4 11.5 %collective-permute-start.15 = (f32[132,2]{1,0:T(8,128)S(1)}, f32[132,2]{1,0:T(8,128)S(1)}, u32[]{:S(2)}, u32[]{:S(2)}) collective-permute-start(f32[132,2]{1,0:T(8,128)S(1)} %get-tuple-element.91), channel_id=1, source_target_pairs={{1,0},{2,1},{3,2},{4,3},{5,4},{6,5},{7,6},{8,7},{9,8},{10,9},{11,1... | collective-permute-start | bytes 3176 | tf_op jit(solution)/shard_map/ppermute | solution.py:28
  81.1 4.4 %collective-permute-start.14 = (f32[132,2]{1,0:T(8,128)S(1)}, f32[132,2]{1,0:T(8,128)S(1)}, u32[]{:S(2)}, u32[]{:S(2)}) collective-permute-start(f32[132,2]{1,0:T(8,128)S(1)} %get-tuple-element.90), channel_id=1, source_target_pairs={{0,1},{1,2},{2,3},{3,4},{4,5},{5,6},{6,7},{7,8},{8,9},{9,10},{10,1... | collective-permute-start | bytes 3176 | tf_op jit(solution)/shard_map/ppermute | solution.py:26
  86.3 6.0 %scatter_custom_fusion = f32[65536]{0:T(1024)S(1)} fusion(s32[1024]{0:T(1024)S(1)} %fusion.119, f32[1024]{0:T(1024)S(1)} %bitcast.238, f32[]{:T(128)} %constant.364.clone.1), kind=kCustom, calls=%fused_computation.227 | custom fusion | flops 1024 | bytes 262148 | tf_op jit(solution)/shard_map/scatter-add | solution.py:129
  95.9 6.2 %gather_fusion.1 = f32[1024]{0:T(1024)S(1)} fusion(f32[65536]{0:T(1024)S(1)} %bitcast.196, s32[1024]{0:T(1024)S(1)} %broadcast_clamp_fusion), kind=kCustom, calls=%fused_computation.1 | custom fusion | bytes 12288 | tf_op jit(solution)/shard_map/gather | solution.py:127
  112.2 7.3 %collective-permute-start.5 = (f32[2,10,1,128]{3,2,1,0:T(1,128)S(1)}, f32[2,10,1,128]{3,2,1,0:T(1,128)S(1)}, u32[]{:S(2)}, u32[]{:S(2)}) collective-permute-start(f32[2,10,1,128]{3,2,1,0:T(1,128)S(1)} %get-tuple-element.138), channel_id=1, source_target_pairs={{0,1},{1,2},{2,3},{3,4},{4,5},{5,6},{6,7},{7,8},{8,9},{9,10},{10,1... | collective-permute-start | bytes 30728 | tf_op jit(solution)/shard_map/ppermute | solution.py:26
  121.5 7.5 %collective-permute-start.18 = (f32[132,2]{1,0:T(8,128)S(1)}, f32[132,2]{1,0:T(8,128)S(1)}, u32[]{:S(2)}, u32[]{:S(2)}) collective-permute-start(f32[132,2]{1,0:T(8,128)S(1)} %get-tuple-element.88), channel_id=1, source_target_pairs={{0,1},{1,2},{2,3},{3,4},{4,5},{5,6},{6,7},{7,8},{8,9},{9,10},{10,1... | collective-permute-start | bytes 3176 | tf_op jit(solution)/shard_map/ppermute | solution.py:26
  129.0 21.8 %multiply_reduce_fusion.21 = (f32[8,8,128]{2,1,0:T(8,128)S(1)}, f32[8,8,128]{2,1,0:T(8,128)S(1)}, f32[8,8,128]{2,1,0:T(8,128)S(1)}, f32[8,8,128]{2,1,0:T(8,128)S(1)}) fusion(f32[8,8,128]{2,1,0:T(8,128)S(1)} %get-tuple-element.151, f32[8,8,128]{2,1,0:T(8,128)S(1)} %get-tuple-element.149, f32[128,128]{1,0:T(8,128)S(1)} %get-tuple-element.202, ...), kind=kLoop, calls=%fused_computation.68 | loop fusion | flops 67076096 | bytes 786944 | tf_op jit(solution)/shard_map/reduce_sum | solution.py:63
  154.0 21.8 %multiply_reduce_fusion.23 = (f32[8,8,128]{2,1,0:T(8,128)S(1)}, f32[8,8,128]{2,1,0:T(8,128)S(1)}, f32[8,8,128]{2,1,0:T(8,128)S(1)}, f32[8,8,128]{2,1,0:T(8,128)S(1)}) fusion(f32[8,8,128]{2,1,0:T(8,128)S(1)} %get-tuple-element.131, f32[8,8,128]{2,1,0:T(8,128)S(1)} %get-tuple-element.125, f32[128,128]{1,0:T(8,128)S(1)} %get-tuple-element.202, ...), kind=kLoop, calls=%fused_computation.77 | loop fusion | flops 67076096 | bytes 786944 | tf_op jit(solution)/shard_map/reduce_sum | solution.py:63
  175.9 21.8 %multiply_reduce_fusion.31 = (f32[8,8,128]{2,1,0:T(8,128)S(1)}, f32[8,8,128]{2,1,0:T(8,128)S(1)}, f32[8,8,128]{2,1,0:T(8,128)S(1)}, f32[8,8,128]{2,1,0:T(8,128)S(1)}) fusion(f32[8,8,128]{2,1,0:T(8,128)S(1)} %get-tuple-element.115, f32[8,8,128]{2,1,0:T(8,128)S(1)} %get-tuple-element.109, f32[8,8,128]{2,1,0:T(8,128)S(1)} %get-tuple-element.167, ...), kind=kLoop, calls=%fused_computation.113 | loop fusion | flops 67076096 | bytes 786944 | tf_op jit(solution)/shard_map/reduce_sum | solution.py:63
  197.7 32.4 %multiply_reduce_fusion.19 = (f32[8,8,128]{2,1,0:T(8,128)S(1)}, f32[8,8,128]{2,1,0:T(8,128)S(1)}, f32[8,8,128]{2,1,0:T(8,128)S(1)}, f32[8,8,128]{2,1,0:T(8,128)S(1)}) fusion(f32[8,8,128]{2,1,0:T(8,128)S(1)} %get-tuple-element.119, f32[8,8,128]{2,1,0:T(8,128)S(1)} %get-tuple-element.113, f32[128,128]{1,0:T(8,128)S(1)} %get-tuple-element.202, ...), kind=kLoop, calls=%fused_computation.59 | loop fusion | flops 67076096 | bytes 786944 | tf_op jit(solution)/shard_map/reduce_sum | solution.py:63
  237.6 14.9 %psum.30 = f32[8,128]{1,0:T(8,128)S(1)} all-reduce(f32[8,128]{1,0:T(8,128)S(1)} %fusion.89), channel_id=1, replica_groups=mesh['gx'=8,'gy'=16] {'gx'}, use_global_device_ids=true, to_apply=%region_39.40 | all-reduce | flops 1024 | bytes 8192 | tf_op jit(solution)/shard_map/psum | solution.py:37
  252.5 6.0 %scatter_custom_fusion.1 = f32[65536]{0:T(1024)S(1)} fusion(s32[1024]{0:T(1024)S(1)} %fusion.119, f32[1024]{0:T(1024)S(1)} %bitcast.236, f32[]{:T(128)} %constant.364.clone.1), kind=kCustom, calls=%fused_computation.225 | custom fusion | flops 1024 | bytes 262148 | tf_op jit(solution)/shard_map/scatter-add | solution.py:129
  259.7 15.9 %psum.31 = f32[8,128]{1,0:T(8,128)S(1)} all-reduce(f32[8,128]{1,0:T(8,128)S(1)} %fusion.92), channel_id=1, replica_groups=mesh['gx'=8,'gy'=16] {'gx'}, use_global_device_ids=true, to_apply=%region_41.42 | all-reduce | flops 1024 | bytes 8192 | tf_op jit(solution)/shard_map/psum | solution.py:131
  275.7 10.1 %collective-permute-start.11 = (f32[2,10,1,128]{3,2,1,0:T(1,128)S(1)}, f32[2,10,1,128]{3,2,1,0:T(1,128)S(1)}, u32[]{:S(2)}, u32[]{:S(2)}) collective-permute-start(f32[2,10,1,128]{3,2,1,0:T(1,128)S(1)} %get-tuple-element.134), channel_id=1, source_target_pairs={{1,0},{2,1},{3,2},{4,3},{5,4},{6,5},{7,6},{8,7},{9,8},{10,9},{11,1... | collective-permute-start | bytes 30728 | tf_op jit(solution)/shard_map/ppermute | solution.py:28
  285.8 6.5 %collective-permute-start.10 = (f32[2,10,1,128]{3,2,1,0:T(1,128)S(1)}, f32[2,10,1,128]{3,2,1,0:T(1,128)S(1)}, u32[]{:S(2)}, u32[]{:S(2)}) collective-permute-start(f32[2,10,1,128]{3,2,1,0:T(1,128)S(1)} %get-tuple-element.135), channel_id=1, source_target_pairs={{0,1},{1,2},{2,3},{3,4},{4,5},{5,6},{6,7},{7,8},{8,9},{9,10},{10,1... | collective-permute-start | bytes 30728 | tf_op jit(solution)/shard_map/ppermute | solution.py:26
  292.3 21.7 %multiply_reduce_fusion.9 = (f32[8,8,128]{2,1,0:T(8,128)S(1)}, f32[8,8,128]{2,1,0:T(8,128)S(1)}, f32[8,8,128]{2,1,0:T(8,128)S(1)}, f32[8,8,128]{2,1,0:T(8,128)S(1)}) fusion(f32[8,8,128]{2,1,0:T(8,128)S(1)} %get-tuple-element.155, f32[8,8,128]{2,1,0:T(8,128)S(1)} %get-tuple-element.165, f32[128,128]{1,0:T(8,128)S(1)} %get-tuple-element.200, ...), kind=kLoop, calls=%fused_computation.34 | loop fusion | flops 67076096 | bytes 655872 | tf_op jit(solution)/shard_map/reduce_sum | solution.py:63
  314.2 11.1 %multiply_reduce_fusion.17 = (f32[8,8,128]{2,1,0:T(8,128)S(1)}, f32[8,8,128]{2,1,0:T(8,128)S(1)}) fusion(f32[8,8,128]{2,1,0:T(8,128)S(1)} %get-tuple-element.155, f32[8,8,128]{2,1,0:T(8,128)S(1)} %get-tuple-element.107, f32[8,8,128]{2,1,0:T(8,128)S(1)} %get-tuple-element.165, f32[8,8,128]{2,1,0:T(8,128)S(1)} %get-tuple-element.121, ...), kind=kLoop, calls=%fused_computation.54 | loop fusion | flops 33538048 | bytes 524544 | tf_op jit(solution)/shard_map/reduce_sum | solution.py:63
  325.3 22.0 %multiply_reduce_fusion.7 = (f32[8,8,128]{2,1,0:T(8,128)S(1)}, f32[8,8,128]{2,1,0:T(8,128)S(1)}, f32[8,8,128]{2,1,0:T(8,128)S(1)}, f32[8,8,128]{2,1,0:T(8,128)S(1)}) fusion(f32[8,8,128]{2,1,0:T(8,128)S(1)} %get-tuple-element.99, f32[8,8,128]{2,1,0:T(8,128)S(1)} %get-tuple-element.155, f32[8,8,128]{2,1,0:T(8,128)S(1)} %get-tuple-element.108, ...), kind=kLoop, calls=%fused_computation.29 | loop fusion | flops 67076096 | bytes 786944 | tf_op jit(solution)/shard_map/reduce_sum | solution.py:63
  347.3 21.8 %multiply_reduce_fusion.5 = (f32[8,8,128]{2,1,0:T(8,128)S(1)}, f32[8,8,128]{2,1,0:T(8,128)S(1)}, f32[8,8,128]{2,1,0:T(8,128)S(1)}, f32[8,8,128]{2,1,0:T(8,128)S(1)}) fusion(f32[8,8,128]{2,1,0:T(8,128)S(1)} %get-tuple-element.104, f32[8,8,128]{2,1,0:T(8,128)S(1)} %get-tuple-element.155, f32[8,8,128]{2,1,0:T(8,128)S(1)} %get-tuple-element.125, ...), kind=kLoop, calls=%fused_computation.24 | loop fusion | flops 67076096 | bytes 786944 | tf_op jit(solution)/shard_map/reduce_sum | solution.py:63
  369.1 22.0 %multiply_reduce_fusion.1 = (f32[8,8,128]{2,1,0:T(8,128)S(1)}, f32[8,8,128]{2,1,0:T(8,128)S(1)}, f32[8,8,128]{2,1,0:T(8,128)S(1)}, f32[8,8,128]{2,1,0:T(8,128)S(1)}) fusion(f32[8,8,128]{2,1,0:T(8,128)S(1)} %get-tuple-element.97, f32[8,8,128]{2,1,0:T(8,128)S(1)} %get-tuple-element.155, f32[8,8,128]{2,1,0:T(8,128)S(1)} %get-tuple-element.113, ...), kind=kLoop, calls=%fused_computation.14 | loop fusion | flops 67076096 | bytes 786944 | tf_op jit(solution)/shard_map/reduce_sum | solution.py:63
  (129 shorter events, 51.0 us)
Async XLA Ops:
  0.6 17.6 %copy-start.6 = (s32[8,128]{1,0:T(8,128)S(1)}, s32[8,128]{1,0:T(8,128)}, u32[]{:S(2)}) copy-start(s32[8,128]{1,0:T(8,128)} %param.16) | copy-start | bytes 12292
  0.6 17.7 %copy-start.1 = (s32[8,8,9]{2,1,0:T(8,128)S(1)}, s32[8,8,9]{2,1,0:T(8,128)}, u32[]{:S(2)}) copy-start(s32[8,8,9]{2,1,0:T(8,128)} %param.15) | copy-start | bytes 6916
  1.4 104.8 %collective-permute-start.3 = (f32[2,1,8,128]{3,2,1,0:T(8,128)S(1)}, f32[2,1,8,128]{3,2,1,0:T(8,128)S(1)}, u32[]{:S(2)}, u32[]{:S(2)}) collective-permute-start(f32[2,1,8,128]{3,2,1,0:T(8,128)S(1)} %get-tuple-element.171), channel_id=1, source_target_pairs={{0,16},{16,32},{32,48},{48,64},{64,80},{80,96},{96,112},{1,17},{17... | collective-permute-start | bytes 24584 | tf_op jit(solution)/shard_map/ppermute | solution.py:26
  4.6 103.6 %collective-permute-start.4 = (f32[2,1,8,128]{3,2,1,0:T(8,128)S(1)}, f32[2,1,8,128]{3,2,1,0:T(8,128)S(1)}, u32[]{:S(2)}, u32[]{:S(2)}) collective-permute-start(f32[2,1,8,128]{3,2,1,0:T(8,128)S(1)} %get-tuple-element.170), channel_id=1, source_target_pairs={{16,0},{32,16},{48,32},{64,48},{80,64},{96,80},{112,96},{17,1},{33... | collective-permute-start | bytes 24584 | tf_op jit(solution)/shard_map/ppermute | solution.py:28
  7.4 102.8 %collective-permute-start = (f32[2,1,8,128]{3,2,1,0:T(8,128)S(1)}, f32[2,1,8,128]{3,2,1,0:T(8,128)S(1)}, u32[]{:S(2)}, u32[]{:S(2)}) collective-permute-start(f32[2,1,8,128]{3,2,1,0:T(8,128)S(1)} %get-tuple-element.169), channel_id=1, source_target_pairs={{0,16},{16,32},{32,48},{48,64},{64,80},{80,96},{96,112},{1,17},{17... | collective-permute-start | bytes 24584 | tf_op jit(solution)/shard_map/ppermute | solution.py:26
  11.3 58.0 %collective-permute-start.13 = (f32[2,512]{1,0:T(2,128)S(1)}, f32[2,512]{1,0:T(2,128)S(1)}, u32[]{:S(2)}, u32[]{:S(2)}) collective-permute-start(f32[2,512]{1,0:T(2,128)S(1)} %get-tuple-element.95), channel_id=1, source_target_pairs={{16,0},{32,16},{48,32},{64,48},{80,64},{96,80},{112,96},{17,1},{33... | collective-permute-start | bytes 12296 | tf_op jit(solution)/shard_map/ppermute | solution.py:28
  14.2 55.1 %collective-permute-start.12 = (f32[2,512]{1,0:T(2,128)S(1)}, f32[2,512]{1,0:T(2,128)S(1)}, u32[]{:S(2)}, u32[]{:S(2)}) collective-permute-start(f32[2,512]{1,0:T(2,128)S(1)} %get-tuple-element.94), channel_id=1, source_target_pairs={{0,16},{16,32},{32,48},{48,64},{64,80},{80,96},{96,112},{1,17},{17... | collective-permute-start | bytes 12296 | tf_op jit(solution)/shard_map/ppermute | solution.py:26
  18.3 16.6 %copy-start = (f32[128,512]{1,0:T(8,128)S(1)}, f32[128,512]{1,0:T(8,128)}, u32[]{:S(2)}) copy-start(f32[128,512]{1,0:T(8,128)} %param.18) | copy-start | bytes 786436
  69.4 22.9 %collective-permute-start.15 = (f32[132,2]{1,0:T(8,128)S(1)}, f32[132,2]{1,0:T(8,128)S(1)}, u32[]{:S(2)}, u32[]{:S(2)}) collective-permute-start(f32[132,2]{1,0:T(8,128)S(1)} %get-tuple-element.91), channel_id=1, source_target_pairs={{1,0},{2,1},{3,2},{4,3},{5,4},{6,5},{7,6},{8,7},{9,8},{10,9},{11,1... | collective-permute-start | bytes 3176 | tf_op jit(solution)/shard_map/ppermute | solution.py:28
  81.1 13.3 %collective-permute-start.14 = (f32[132,2]{1,0:T(8,128)S(1)}, f32[132,2]{1,0:T(8,128)S(1)}, u32[]{:S(2)}, u32[]{:S(2)}) collective-permute-start(f32[132,2]{1,0:T(8,128)S(1)} %get-tuple-element.90), channel_id=1, source_target_pairs={{0,1},{1,2},{2,3},{3,4},{4,5},{5,6},{6,7},{7,8},{8,9},{9,10},{10,1... | collective-permute-start | bytes 3176 | tf_op jit(solution)/shard_map/ppermute | solution.py:26
  92.4 17.8 %collective-permute-start.1 = (f32[2,1,8,128]{3,2,1,0:T(8,128)S(1)}, f32[2,1,8,128]{3,2,1,0:T(8,128)S(1)}, u32[]{:S(2)}, u32[]{:S(2)}) collective-permute-start(f32[2,1,8,128]{3,2,1,0:T(8,128)S(1)} %get-tuple-element.168), channel_id=1, source_target_pairs={{16,0},{32,16},{48,32},{64,48},{80,64},{96,80},{112,96},{17,1},{33... | collective-permute-start | bytes 24584 | tf_op jit(solution)/shard_map/ppermute | solution.py:28
  102.1 8.1 %copy-start.3 = (f32[2,8,8,128]{3,2,1,0:T(8,128)S(1)}, f32[2,8,8,128]{3,2,1,0:T(8,128)}, u32[]{:S(2)}) copy-start(f32[2,8,8,128]{3,2,1,0:T(8,128)} %param.14) | copy-start | bytes 196612
  102.1 17.4 %collective-permute-start.17 = (f32[2,512]{1,0:T(2,128)S(1)}, f32[2,512]{1,0:T(2,128)S(1)}, u32[]{:S(2)}, u32[]{:S(2)}) collective-permute-start(f32[2,512]{1,0:T(2,128)S(1)} %get-tuple-element.93), channel_id=1, source_target_pairs={{16,0},{32,16},{48,32},{64,48},{80,64},{96,80},{112,96},{17,1},{33... | collective-permute-start | bytes 12296 | tf_op jit(solution)/shard_map/ppermute | solution.py:28
  106.2 13.3 %collective-permute-start.16 = (f32[2,512]{1,0:T(2,128)S(1)}, f32[2,512]{1,0:T(2,128)S(1)}, u32[]{:S(2)}, u32[]{:S(2)}) collective-permute-start(f32[2,512]{1,0:T(2,128)S(1)} %get-tuple-element.92), channel_id=1, source_target_pairs={{0,16},{16,32},{32,48},{48,64},{64,80},{80,96},{96,112},{1,17},{17... | collective-permute-start | bytes 12296 | tf_op jit(solution)/shard_map/ppermute | solution.py:26
  108.2 67.6 %collective-permute-start.7 = (f32[2,10,1,128]{3,2,1,0:T(1,128)S(1)}, f32[2,10,1,128]{3,2,1,0:T(1,128)S(1)}, u32[]{:S(2)}, u32[]{:S(2)}) collective-permute-start(f32[2,10,1,128]{3,2,1,0:T(1,128)S(1)} %get-tuple-element.139), channel_id=1, source_target_pairs={{1,0},{2,1},{3,2},{4,3},{5,4},{6,5},{7,6},{8,7},{9,8},{10,9},{11,1... | collective-permute-start | bytes 30728 | tf_op jit(solution)/shard_map/ppermute | solution.py:28
  110.3 65.6 %collective-permute-start.6 = (f32[2,10,1,128]{3,2,1,0:T(1,128)S(1)}, f32[2,10,1,128]{3,2,1,0:T(1,128)S(1)}, u32[]{:S(2)}, u32[]{:S(2)}) collective-permute-start(f32[2,10,1,128]{3,2,1,0:T(1,128)S(1)} %get-tuple-element.137), channel_id=1, source_target_pairs={{1,0},{2,1},{3,2},{4,3},{5,4},{6,5},{7,6},{8,7},{9,8},{10,9},{11,1... | collective-permute-start | bytes 30728 | tf_op jit(solution)/shard_map/ppermute | solution.py:28
  112.2 41.6 %collective-permute-start.5 = (f32[2,10,1,128]{3,2,1,0:T(1,128)S(1)}, f32[2,10,1,128]{3,2,1,0:T(1,128)S(1)}, u32[]{:S(2)}, u32[]{:S(2)}) collective-permute-start(f32[2,10,1,128]{3,2,1,0:T(1,128)S(1)} %get-tuple-element.138), channel_id=1, source_target_pairs={{0,1},{1,2},{2,3},{3,4},{4,5},{5,6},{6,7},{7,8},{8,9},{9,10},{10,1... | collective-permute-start | bytes 30728 | tf_op jit(solution)/shard_map/ppermute | solution.py:26
  119.6 31.3 %collective-permute-start.19 = (f32[132,2]{1,0:T(8,128)S(1)}, f32[132,2]{1,0:T(8,128)S(1)}, u32[]{:S(2)}, u32[]{:S(2)}) collective-permute-start(f32[132,2]{1,0:T(8,128)S(1)} %get-tuple-element.89), channel_id=1, source_target_pairs={{1,0},{2,1},{3,2},{4,3},{5,4},{6,5},{7,6},{8,7},{9,8},{10,9},{11,1... | collective-permute-start | bytes 3176 | tf_op jit(solution)/shard_map/ppermute | solution.py:28
  121.5 31.6 %collective-permute-start.18 = (f32[132,2]{1,0:T(8,128)S(1)}, f32[132,2]{1,0:T(8,128)S(1)}, u32[]{:S(2)}, u32[]{:S(2)}) collective-permute-start(f32[132,2]{1,0:T(8,128)S(1)} %get-tuple-element.88), channel_id=1, source_target_pairs={{0,1},{1,2},{2,3},{3,4},{4,5},{5,6},{6,7},{7,8},{8,9},{9,10},{10,1... | collective-permute-start | bytes 3176 | tf_op jit(solution)/shard_map/ppermute | solution.py:26
  150.9 3.1 collective-permute-start.2
  232.3 43.4 %collective-permute-start.9 = (f32[2,1,8,128]{3,2,1,0:T(8,128)S(1)}, f32[2,1,8,128]{3,2,1,0:T(8,128)S(1)}, u32[]{:S(2)}, u32[]{:S(2)}) collective-permute-start(f32[2,1,8,128]{3,2,1,0:T(8,128)S(1)} %get-tuple-element.157), channel_id=1, source_target_pairs={{16,0},{32,16},{48,32},{64,48},{80,64},{96,80},{112,96},{17,1},{33... | collective-permute-start | bytes 24584 | tf_op jit(solution)/shard_map/ppermute | solution.py:28
  235.7 40.0 %collective-permute-start.8 = (f32[2,1,8,128]{3,2,1,0:T(8,128)S(1)}, f32[2,1,8,128]{3,2,1,0:T(8,128)S(1)}, u32[]{:S(2)}, u32[]{:S(2)}) collective-permute-start(f32[2,1,8,128]{3,2,1,0:T(8,128)S(1)} %get-tuple-element.156), channel_id=1, source_target_pairs={{0,16},{16,32},{32,48},{48,64},{64,80},{80,96},{96,112},{1,17},{17... | collective-permute-start | bytes 24584 | tf_op jit(solution)/shard_map/ppermute | solution.py:26
  275.7 38.4 %collective-permute-start.11 = (f32[2,10,1,128]{3,2,1,0:T(1,128)S(1)}, f32[2,10,1,128]{3,2,1,0:T(1,128)S(1)}, u32[]{:S(2)}, u32[]{:S(2)}) collective-permute-start(f32[2,10,1,128]{3,2,1,0:T(1,128)S(1)} %get-tuple-element.134), channel_id=1, source_target_pairs={{1,0},{2,1},{3,2},{4,3},{5,4},{6,5},{7,6},{8,7},{9,8},{10,9},{11,1... | collective-permute-start | bytes 30728 | tf_op jit(solution)/shard_map/ppermute | solution.py:28
  285.8 28.3 %collective-permute-start.10 = (f32[2,10,1,128]{3,2,1,0:T(1,128)S(1)}, f32[2,10,1,128]{3,2,1,0:T(1,128)S(1)}, u32[]{:S(2)}, u32[]{:S(2)}) collective-permute-start(f32[2,10,1,128]{3,2,1,0:T(1,128)S(1)} %get-tuple-element.135), channel_id=1, source_target_pairs={{0,1},{1,2},{2,3},{3,4},{4,5},{5,6},{6,7},{7,8},{8,9},{9,10},{10,1... | collective-permute-start | bytes 30728 | tf_op jit(solution)/shard_map/ppermute | solution.py:26
  (5 other events, 11.4 us)
where the time goes:
time: 401 us; the launch traced here: 394 us
  other arithmetic  229 us (57%)
  starting transfers between devices  82.2 us (20%)
  blocking collectives  62.5 us (16%)
  local copies, waits for them, and re-layouts  18.8 us (5%)
    reduce_sum x10, other arithmetic, pair_force(): jnp.sum(factor * now_x, axis=-1)  207 us
    ppermute x10, starting transfers between devices, extended(): lax.ppermute(head, axis, [((i + 1) % count, i) for i in range(ends)])  41.7 us
    ppermute x10, starting transfers between devices, extended(): lax.ppermute(tail, axis, [(i, (i + 1) % count) for i in range(ends)])  40.4 us
    psum x2, blocking collectives, on_device(): my_pushes = lax.psum(pushes, 'gx') * front_flag  32 us
    psum x2, blocking collectives, spread(): return lax.psum(jnp.where(mine, array, jnp.zeros_like(array)), axis)  30.5 us
    gather x2, local copies, waits for them, and re-layouts, on_device(): reached = shell_deflection.reshape(-1)[local_ids].reshape(gaps.shape)  12.3 us
    scatter-add x2, other arithmetic, on_device(): jax.ops.segment_sum(pushes.reshape(-1), local_ids, num_segments=node_count)  12 us
  transfers between devices with their start and end apart: 20, of which 1 were waited for; matrix products, arithmetic and copies ran while one was open for 28% of the time, Pallas kernels for 0%

commit v1 on v0

--- a/solution.py
+++ b/solution.py
@@ -128,7 +128,7 @@
         pushes = jnp.where(owned, PENALTY * jnp.maximum(gaps - reached, 0.0), 0.0)
         loading = jax.ops.segment_sum(pushes.reshape(-1), local_ids, num_segments=node_count)
         loading = loading.reshape(shell_rows, shell_cols)
-        my_pushes = lax.psum(pushes, "gx") * front_flag
+        my_pushes = jnp.sum(lax.all_gather(pushes, "gx"), axis=0) * front_flag
         forces = forces.at[0, -1].add(-my_pushes)
         shell_padded = extended(shell_deflection, (("gx", 0), ("gy", 1)), 2)
         bending = laplace(laplace(shell_padded))

time: 401 us -> 425 us (1.060)
  the two profiles are of different devices: /device:TPU:47 before, /device:TPU:39 now
where the time goes in v1:
time: 425 us; the launch traced here: 419 us
  other arithmetic  229 us (54%)
  starting transfers between devices  92.7 us (22%)
  blocking collectives  75.8 us (18%)
  local copies, waits for them, and re-layouts  19.2 us (5%)
    reduce_sum x10, other arithmetic, pair_force(): jnp.sum(factor * now_x, axis=-1)  207 us
    ppermute x10, starting transfers between devices, extended(): lax.ppermute(head, axis, [((i + 1) % count, i) for i in range(ends)])  54 us
    all_gather x2, blocking collectives, on_device(): my_pushes = jnp.sum(lax.all_gather(pushes, 'gx'), axis=0) * front_flag  43.8 us
    ppermute x10, starting transfers between devices, extended(): lax.ppermute(tail, axis, [(i, (i + 1) % count) for i in range(ends)])  38.7 us
    psum x2, blocking collectives, spread(): return lax.psum(jnp.where(mine, array, jnp.zeros_like(array)), axis)  32.1 us
    gather x2, local copies, waits for them, and re-layouts, on_device(): reached = shell_deflection.reshape(-1)[local_ids].reshape(gaps.shape)  12.3 us
    scatter-add x2, other arithmetic, on_device(): jax.ops.segment_sum(pushes.reshape(-1), local_ids, num_segments=node_count)  12 us
  transfers between devices with their start and end apart: 20, of which 1 were waited for; matrix products, arithmetic and copies ran while one was open for 26% of the time, Pallas kernels for 0%

profile of v1, /device:TPU:39, one launch (start us, length us, event | category | flops | bytes accessed | tf_op | source)
XLA Modules:
  0.0 418.7 jit_solution(12512808589588202777)
XLA Ops:
  22.1 16.0 %psum.14 = f32[8,128]{1,0:T(8,128)S(1)} all-reduce(f32[8,128]{1,0:T(8,128)S(1)} %fusion.96), channel_id=1, replica_groups=mesh['gx'=8,'gy'=16] {'gx'}, use_global_device_ids=true, to_apply=%region_19.20 | all-reduce | flops 1024 | bytes 8192 | tf_op jit(solution)/shard_map/psum | solution.py:37
  38.2 6.2 %gather_fusion = f32[1024]{0:T(1024)S(1)} fusion(f32[65536]{0:T(1024)S(1)} %bitcast.199, s32[1024]{0:T(1024)S(1)} %broadcast_clamp_fusion), kind=kCustom, calls=%fused_computation | custom fusion | bytes 12288 | tf_op jit(solution)/shard_map/gather | solution.py:127
  44.4 21.9 %all-gather = f32[64,128]{1,0:T(8,128)S(1)} all-gather(f32[8,128]{1,0:T(8,128)S(1)} %get-tuple-element.86), channel_id=2, replica_groups=mesh['gx'=8,'gy'=16] {'gx'}, dimensions={0}, use_global_device_ids=true | all-gather | bytes 36864 | tf_op jit(solution)/shard_map/all_gather | solution.py:131
  67.4 10.9 %multiply_reduce_fusion.27 = (f32[8,8,128]{2,1,0:T(8,128)S(1)}, f32[8,8,128]{2,1,0:T(8,128)S(1)}) fusion(f32[8,8,128]{2,1,0:T(8,128)S(1)} %get-tuple-element.167, f32[8,8,128]{2,1,0:T(8,128)S(1)} %get-tuple-element.165, f32[128,128]{1,0:T(8,128)S(1)} %get-tuple-element.200, f32[8,8,128]{2,1,0:T(8,128)S(1)} %get-tuple-element.166, ...), kind=kLoop, calls=%fused_computation.95 | loop fusion | flops 33538048 | bytes 393472 | tf_op jit(solution)/shard_map/reduce_sum | solution.py:63
  79.0 14.1 %collective-permute-start.15 = (f32[132,2]{1,0:T(8,128)S(1)}, f32[132,2]{1,0:T(8,128)S(1)}, u32[]{:S(2)}, u32[]{:S(2)}) collective-permute-start(f32[132,2]{1,0:T(8,128)S(1)} %get-tuple-element.91), channel_id=1, source_target_pairs={{1,0},{2,1},{3,2},{4,3},{5,4},{6,5},{7,6},{8,7},{9,8},{10,9},{11,1... | collective-permute-start | bytes 3176 | tf_op jit(solution)/shard_map/ppermute | solution.py:28
  98.5 6.0 %scatter_custom_fusion = f32[65536]{0:T(1024)S(1)} fusion(s32[1024]{0:T(1024)S(1)} %fusion.119, f32[1024]{0:T(1024)S(1)} %bitcast.240, f32[]{:T(128)} %constant.364.clone.1), kind=kCustom, calls=%fused_computation.227 | custom fusion | flops 1024 | bytes 262148 | tf_op jit(solution)/shard_map/scatter-add | solution.py:129
  108.5 6.2 %gather_fusion.1 = f32[1024]{0:T(1024)S(1)} fusion(f32[65536]{0:T(1024)S(1)} %bitcast.200, s32[1024]{0:T(1024)S(1)} %broadcast_clamp_fusion), kind=kCustom, calls=%fused_computation.1 | custom fusion | bytes 12288 | tf_op jit(solution)/shard_map/gather | solution.py:127
  124.4 7.3 %collective-permute-start.5 = (f32[2,10,1,128]{3,2,1,0:T(1,128)S(1)}, f32[2,10,1,128]{3,2,1,0:T(1,128)S(1)}, u32[]{:S(2)}, u32[]{:S(2)}) collective-permute-start(f32[2,10,1,128]{3,2,1,0:T(1,128)S(1)} %get-tuple-element.138), channel_id=1, source_target_pairs={{0,1},{1,2},{2,3},{3,4},{4,5},{5,6},{6,7},{7,8},{8,9},{9,10},{10,1... | collective-permute-start | bytes 30728 | tf_op jit(solution)/shard_map/ppermute | solution.py:26
  133.7 7.5 %collective-permute-start.18 = (f32[132,2]{1,0:T(8,128)S(1)}, f32[132,2]{1,0:T(8,128)S(1)}, u32[]{:S(2)}, u32[]{:S(2)}) collective-permute-start(f32[132,2]{1,0:T(8,128)S(1)} %get-tuple-element.88), channel_id=1, source_target_pairs={{0,1},{1,2},{2,3},{3,4},{4,5},{5,6},{6,7},{7,8},{8,9},{9,10},{10,1... | collective-permute-start | bytes 3176 | tf_op jit(solution)/shard_map/ppermute | solution.py:26
  141.2 21.8 %multiply_reduce_fusion.21 = (f32[8,8,128]{2,1,0:T(8,128)S(1)}, f32[8,8,128]{2,1,0:T(8,128)S(1)}, f32[8,8,128]{2,1,0:T(8,128)S(1)}, f32[8,8,128]{2,1,0:T(8,128)S(1)}) fusion(f32[8,8,128]{2,1,0:T(8,128)S(1)} %get-tuple-element.151, f32[8,8,128]{2,1,0:T(8,128)S(1)} %get-tuple-element.149, f32[128,128]{1,0:T(8,128)S(1)} %get-tuple-element.202, ...), kind=kLoop, calls=%fused_computation.68 | loop fusion | flops 67076096 | bytes 786944 | tf_op jit(solution)/shard_map/reduce_sum | solution.py:63
  166.2 21.8 %multiply_reduce_fusion.23 = (f32[8,8,128]{2,1,0:T(8,128)S(1)}, f32[8,8,128]{2,1,0:T(8,128)S(1)}, f32[8,8,128]{2,1,0:T(8,128)S(1)}, f32[8,8,128]{2,1,0:T(8,128)S(1)}) fusion(f32[8,8,128]{2,1,0:T(8,128)S(1)} %get-tuple-element.131, f32[8,8,128]{2,1,0:T(8,128)S(1)} %get-tuple-element.125, f32[128,128]{1,0:T(8,128)S(1)} %get-tuple-element.202, ...), kind=kLoop, calls=%fused_computation.77 | loop fusion | flops 67076096 | bytes 786944 | tf_op jit(solution)/shard_map/reduce_sum | solution.py:63
  188.1 21.8 %multiply_reduce_fusion.31 = (f32[8,8,128]{2,1,0:T(8,128)S(1)}, f32[8,8,128]{2,1,0:T(8,128)S(1)}, f32[8,8,128]{2,1,0:T(8,128)S(1)}, f32[8,8,128]{2,1,0:T(8,128)S(1)}) fusion(f32[8,8,128]{2,1,0:T(8,128)S(1)} %get-tuple-element.115, f32[8,8,128]{2,1,0:T(8,128)S(1)} %get-tuple-element.109, f32[8,8,128]{2,1,0:T(8,128)S(1)} %get-tuple-element.167, ...), kind=kLoop, calls=%fused_computation.113 | loop fusion | flops 67076096 | bytes 786944 | tf_op jit(solution)/shard_map/reduce_sum | solution.py:63
  209.9 32.4 %multiply_reduce_fusion.19 = (f32[8,8,128]{2,1,0:T(8,128)S(1)}, f32[8,8,128]{2,1,0:T(8,128)S(1)}, f32[8,8,128]{2,1,0:T(8,128)S(1)}, f32[8,8,128]{2,1,0:T(8,128)S(1)}) fusion(f32[8,8,128]{2,1,0:T(8,128)S(1)} %get-tuple-element.119, f32[8,8,128]{2,1,0:T(8,128)S(1)} %get-tuple-element.113, f32[128,128]{1,0:T(8,128)S(1)} %get-tuple-element.202, ...), kind=kLoop, calls=%fused_computation.59 | loop fusion | flops 67076096 | bytes 786944 | tf_op jit(solution)/shard_map/reduce_sum | solution.py:63
  244.5 5.5 %collective-permute-start.9 = (f32[2,1,8,128]{3,2,1,0:T(8,128)S(1)}, f32[2,1,8,128]{3,2,1,0:T(8,128)S(1)}, u32[]{:S(2)}, u32[]{:S(2)}) collective-permute-start(f32[2,1,8,128]{3,2,1,0:T(8,128)S(1)} %get-tuple-element.157), channel_id=1, source_target_pairs={{16,0},{32,16},{48,32},{64,48},{80,64},{96,80},{112,96},{17,1},{33... | collective-permute-start | bytes 24584 | tf_op jit(solution)/shard_map/ppermute | solution.py:28
  251.9 16.0 %psum.15 = f32[8,128]{1,0:T(8,128)S(1)} all-reduce(f32[8,128]{1,0:T(8,128)S(1)} %fusion.89), channel_id=1, replica_groups=mesh['gx'=8,'gy'=16] {'gx'}, use_global_device_ids=true, to_apply=%region_39.40 | all-reduce | flops 1024 | bytes 8192 | tf_op jit(solution)/shard_map/psum | solution.py:37
  268.0 21.9 %all-gather.1 = f32[64,128]{1,0:T(8,128)S(1)} all-gather(f32[8,128]{1,0:T(8,128)S(1)} %fusion.92), channel_id=3, replica_groups=mesh['gx'=8,'gy'=16] {'gx'}, dimensions={0}, use_global_device_ids=true | all-gather | bytes 36864 | tf_op jit(solution)/shard_map/all_gather | solution.py:131
  289.9 6.0 %scatter_custom_fusion.1 = f32[65536]{0:T(1024)S(1)} fusion(s32[1024]{0:T(1024)S(1)} %fusion.119, f32[1024]{0:T(1024)S(1)} %bitcast.239, f32[]{:T(128)} %constant.364.clone.1), kind=kCustom, calls=%fused_computation.225 | custom fusion | flops 1024 | bytes 262148 | tf_op jit(solution)/shard_map/scatter-add | solution.py:129
  297.1 13.0 %collective-permute-start.11 = (f32[2,10,1,128]{3,2,1,0:T(1,128)S(1)}, f32[2,10,1,128]{3,2,1,0:T(1,128)S(1)}, u32[]{:S(2)}, u32[]{:S(2)}) collective-permute-start(f32[2,10,1,128]{3,2,1,0:T(1,128)S(1)} %get-tuple-element.134), channel_id=1, source_target_pairs={{1,0},{2,1},{3,2},{4,3},{5,4},{6,5},{7,6},{8,7},{9,8},{10,9},{11,1... | collective-permute-start | bytes 30728 | tf_op jit(solution)/shard_map/ppermute | solution.py:28
  310.1 6.5 %collective-permute-start.10 = (f32[2,10,1,128]{3,2,1,0:T(1,128)S(1)}, f32[2,10,1,128]{3,2,1,0:T(1,128)S(1)}, u32[]{:S(2)}, u32[]{:S(2)}) collective-permute-start(f32[2,10,1,128]{3,2,1,0:T(1,128)S(1)} %get-tuple-element.135), channel_id=1, source_target_pairs={{0,1},{1,2},{2,3},{3,4},{4,5},{5,6},{6,7},{7,8},{8,9},{9,10},{10,1... | collective-permute-start | bytes 30728 | tf_op jit(solution)/shard_map/ppermute | solution.py:26
  316.6 21.7 %multiply_reduce_fusion.9 = (f32[8,8,128]{2,1,0:T(8,128)S(1)}, f32[8,8,128]{2,1,0:T(8,128)S(1)}, f32[8,8,128]{2,1,0:T(8,128)S(1)}, f32[8,8,128]{2,1,0:T(8,128)S(1)}) fusion(f32[8,8,128]{2,1,0:T(8,128)S(1)} %get-tuple-element.155, f32[8,8,128]{2,1,0:T(8,128)S(1)} %get-tuple-element.165, f32[128,128]{1,0:T(8,128)S(1)} %get-tuple-element.200, ...), kind=kLoop, calls=%fused_computation.34 | loop fusion | flops 67076096 | bytes 655872 | tf_op jit(solution)/shard_map/reduce_sum | solution.py:63
  338.5 11.1 %multiply_reduce_fusion.17 = (f32[8,8,128]{2,1,0:T(8,128)S(1)}, f32[8,8,128]{2,1,0:T(8,128)S(1)}) fusion(f32[8,8,128]{2,1,0:T(8,128)S(1)} %get-tuple-element.155, f32[8,8,128]{2,1,0:T(8,128)S(1)} %get-tuple-element.107, f32[8,8,128]{2,1,0:T(8,128)S(1)} %get-tuple-element.165, f32[8,8,128]{2,1,0:T(8,128)S(1)} %get-tuple-element.121, ...), kind=kLoop, calls=%fused_computation.54 | loop fusion | flops 33538048 | bytes 524544 | tf_op jit(solution)/shard_map/reduce_sum | solution.py:63
  349.6 22.0 %multiply_reduce_fusion.7 = (f32[8,8,128]{2,1,0:T(8,128)S(1)}, f32[8,8,128]{2,1,0:T(8,128)S(1)}, f32[8,8,128]{2,1,0:T(8,128)S(1)}, f32[8,8,128]{2,1,0:T(8,128)S(1)}) fusion(f32[8,8,128]{2,1,0:T(8,128)S(1)} %get-tuple-element.99, f32[8,8,128]{2,1,0:T(8,128)S(1)} %get-tuple-element.155, f32[8,8,128]{2,1,0:T(8,128)S(1)} %get-tuple-element.108, ...), kind=kLoop, calls=%fused_computation.29 | loop fusion | flops 67076096 | bytes 786944 | tf_op jit(solution)/shard_map/reduce_sum | solution.py:63
  371.6 21.8 %multiply_reduce_fusion.5 = (f32[8,8,128]{2,1,0:T(8,128)S(1)}, f32[8,8,128]{2,1,0:T(8,128)S(1)}, f32[8,8,128]{2,1,0:T(8,128)S(1)}, f32[8,8,128]{2,1,0:T(8,128)S(1)}) fusion(f32[8,8,128]{2,1,0:T(8,128)S(1)} %get-tuple-element.104, f32[8,8,128]{2,1,0:T(8,128)S(1)} %get-tuple-element.155, f32[8,8,128]{2,1,0:T(8,128)S(1)} %get-tuple-element.125, ...), kind=kLoop, calls=%fused_computation.24 | loop fusion | flops 67076096 | bytes 786944 | tf_op jit(solution)/shard_map/reduce_sum | solution.py:63
  393.4 22.0 %multiply_reduce_fusion.1 = (f32[8,8,128]{2,1,0:T(8,128)S(1)}, f32[8,8,128]{2,1,0:T(8,128)S(1)}, f32[8,8,128]{2,1,0:T(8,128)S(1)}, f32[8,8,128]{2,1,0:T(8,128)S(1)}) fusion(f32[8,8,128]{2,1,0:T(8,128)S(1)} %get-tuple-element.97, f32[8,8,128]{2,1,0:T(8,128)S(1)} %get-tuple-element.155, f32[8,8,128]{2,1,0:T(8,128)S(1)} %get-tuple-element.113, ...), kind=kLoop, calls=%fused_computation.14 | loop fusion | flops 67076096 | bytes 786944 | tf_op jit(solution)/shard_map/reduce_sum | solution.py:63
  (131 shorter events, 55.3 us)
Async XLA Ops:
  0.6 20.5 %copy-start.6 = (s32[8,128]{1,0:T(8,128)S(1)}, s32[8,128]{1,0:T(8,128)}, u32[]{:S(2)}) copy-start(s32[8,128]{1,0:T(8,128)} %param.16) | copy-start | bytes 12292
  0.6 20.6 %copy-start.1 = (s32[8,8,9]{2,1,0:T(8,128)S(1)}, s32[8,8,9]{2,1,0:T(8,128)}, u32[]{:S(2)}) copy-start(s32[8,8,9]{2,1,0:T(8,128)} %param.15) | copy-start | bytes 6916
  1.4 117.0 %collective-permute-start.3 = (f32[2,1,8,128]{3,2,1,0:T(8,128)S(1)}, f32[2,1,8,128]{3,2,1,0:T(8,128)S(1)}, u32[]{:S(2)}, u32[]{:S(2)}) collective-permute-start(f32[2,1,8,128]{3,2,1,0:T(8,128)S(1)} %get-tuple-element.171), channel_id=1, source_target_pairs={{0,16},{16,32},{32,48},{48,64},{64,80},{80,96},{96,112},{1,17},{17... | collective-permute-start | bytes 24584 | tf_op jit(solution)/shard_map/ppermute | solution.py:26
  4.6 115.8 %collective-permute-start.4 = (f32[2,1,8,128]{3,2,1,0:T(8,128)S(1)}, f32[2,1,8,128]{3,2,1,0:T(8,128)S(1)}, u32[]{:S(2)}, u32[]{:S(2)}) collective-permute-start(f32[2,1,8,128]{3,2,1,0:T(8,128)S(1)} %get-tuple-element.170), channel_id=1, source_target_pairs={{16,0},{32,16},{48,32},{64,48},{80,64},{96,80},{112,96},{17,1},{33... | collective-permute-start | bytes 24584 | tf_op jit(solution)/shard_map/ppermute | solution.py:28
  9.5 112.9 %collective-permute-start = (f32[2,1,8,128]{3,2,1,0:T(8,128)S(1)}, f32[2,1,8,128]{3,2,1,0:T(8,128)S(1)}, u32[]{:S(2)}, u32[]{:S(2)}) collective-permute-start(f32[2,1,8,128]{3,2,1,0:T(8,128)S(1)} %get-tuple-element.169), channel_id=1, source_target_pairs={{0,16},{16,32},{32,48},{48,64},{64,80},{80,96},{96,112},{1,17},{17... | collective-permute-start | bytes 24584 | tf_op jit(solution)/shard_map/ppermute | solution.py:26
  12.2 66.8 %collective-permute-start.13 = (f32[2,512]{1,0:T(2,128)S(1)}, f32[2,512]{1,0:T(2,128)S(1)}, u32[]{:S(2)}, u32[]{:S(2)}) collective-permute-start(f32[2,512]{1,0:T(2,128)S(1)} %get-tuple-element.95), channel_id=1, source_target_pairs={{16,0},{32,16},{48,32},{64,48},{80,64},{96,80},{112,96},{17,1},{33... | collective-permute-start | bytes 12296 | tf_op jit(solution)/shard_map/ppermute | solution.py:28
  17.6 61.3 %collective-permute-start.12 = (f32[2,512]{1,0:T(2,128)S(1)}, f32[2,512]{1,0:T(2,128)S(1)}, u32[]{:S(2)}, u32[]{:S(2)}) collective-permute-start(f32[2,512]{1,0:T(2,128)S(1)} %get-tuple-element.94), channel_id=1, source_target_pairs={{0,16},{16,32},{32,48},{48,64},{64,80},{80,96},{96,112},{1,17},{17... | collective-permute-start | bytes 12296 | tf_op jit(solution)/shard_map/ppermute | solution.py:26
  21.3 16.9 %copy-start = (f32[128,512]{1,0:T(8,128)S(1)}, f32[128,512]{1,0:T(8,128)}, u32[]{:S(2)}) copy-start(f32[128,512]{1,0:T(8,128)} %param.18) | copy-start | bytes 786436
  44.4 22.2 %copy-start.8 = (s32[4]{0:T(128)S(1)}, s32[4]{0:T(128)}, u32[]{:S(2)}) copy-start(s32[4]{0:T(128)} %constant.374.clone.1) | copy-start | bytes 52
  79.0 25.6 %collective-permute-start.15 = (f32[132,2]{1,0:T(8,128)S(1)}, f32[132,2]{1,0:T(8,128)S(1)}, u32[]{:S(2)}, u32[]{:S(2)}) collective-permute-start(f32[132,2]{1,0:T(8,128)S(1)} %get-tuple-element.91), channel_id=1, source_target_pairs={{1,0},{2,1},{3,2},{4,3},{5,4},{6,5},{7,6},{8,7},{9,8},{10,9},{11,1... | collective-permute-start | bytes 3176 | tf_op jit(solution)/shard_map/ppermute | solution.py:28
  93.3 13.6 %collective-permute-start.14 = (f32[132,2]{1,0:T(8,128)S(1)}, f32[132,2]{1,0:T(8,128)S(1)}, u32[]{:S(2)}, u32[]{:S(2)}) collective-permute-start(f32[132,2]{1,0:T(8,128)S(1)} %get-tuple-element.90), channel_id=1, source_target_pairs={{0,1},{1,2},{2,3},{3,4},{4,5},{5,6},{6,7},{7,8},{8,9},{9,10},{10,1... | collective-permute-start | bytes 3176 | tf_op jit(solution)/shard_map/ppermute | solution.py:26
  104.6 17.8 %collective-permute-start.1 = (f32[2,1,8,128]{3,2,1,0:T(8,128)S(1)}, f32[2,1,8,128]{3,2,1,0:T(8,128)S(1)}, u32[]{:S(2)}, u32[]{:S(2)}) collective-permute-start(f32[2,1,8,128]{3,2,1,0:T(8,128)S(1)} %get-tuple-element.168), channel_id=1, source_target_pairs={{16,0},{32,16},{48,32},{64,48},{80,64},{96,80},{112,96},{17,1},{33... | collective-permute-start | bytes 24584 | tf_op jit(solution)/shard_map/ppermute | solution.py:28
  114.6 17.1 %collective-permute-start.17 = (f32[2,512]{1,0:T(2,128)S(1)}, f32[2,512]{1,0:T(2,128)S(1)}, u32[]{:S(2)}, u32[]{:S(2)}) collective-permute-start(f32[2,512]{1,0:T(2,128)S(1)} %get-tuple-element.93), channel_id=1, source_target_pairs={{16,0},{32,16},{48,32},{64,48},{80,64},{96,80},{112,96},{17,1},{33... | collective-permute-start | bytes 12296 | tf_op jit(solution)/shard_map/ppermute | solution.py:28
  118.4 13.3 %collective-permute-start.16 = (f32[2,512]{1,0:T(2,128)S(1)}, f32[2,512]{1,0:T(2,128)S(1)}, u32[]{:S(2)}, u32[]{:S(2)}) collective-permute-start(f32[2,512]{1,0:T(2,128)S(1)} %get-tuple-element.92), channel_id=1, source_target_pairs={{0,16},{16,32},{32,48},{48,64},{64,80},{80,96},{96,112},{1,17},{17... | collective-permute-start | bytes 12296 | tf_op jit(solution)/shard_map/ppermute | solution.py:26
  120.4 67.6 %collective-permute-start.7 = (f32[2,10,1,128]{3,2,1,0:T(1,128)S(1)}, f32[2,10,1,128]{3,2,1,0:T(1,128)S(1)}, u32[]{:S(2)}, u32[]{:S(2)}) collective-permute-start(f32[2,10,1,128]{3,2,1,0:T(1,128)S(1)} %get-tuple-element.139), channel_id=1, source_target_pairs={{1,0},{2,1},{3,2},{4,3},{5,4},{6,5},{7,6},{8,7},{9,8},{10,9},{11,1... | collective-permute-start | bytes 30728 | tf_op jit(solution)/shard_map/ppermute | solution.py:28
  122.5 65.6 %collective-permute-start.6 = (f32[2,10,1,128]{3,2,1,0:T(1,128)S(1)}, f32[2,10,1,128]{3,2,1,0:T(1,128)S(1)}, u32[]{:S(2)}, u32[]{:S(2)}) collective-permute-start(f32[2,10,1,128]{3,2,1,0:T(1,128)S(1)} %get-tuple-element.137), channel_id=1, source_target_pairs={{1,0},{2,1},{3,2},{4,3},{5,4},{6,5},{7,6},{8,7},{9,8},{10,9},{11,1... | collective-permute-start | bytes 30728 | tf_op jit(solution)/shard_map/ppermute | solution.py:28
  124.4 41.6 %collective-permute-start.5 = (f32[2,10,1,128]{3,2,1,0:T(1,128)S(1)}, f32[2,10,1,128]{3,2,1,0:T(1,128)S(1)}, u32[]{:S(2)}, u32[]{:S(2)}) collective-permute-start(f32[2,10,1,128]{3,2,1,0:T(1,128)S(1)} %get-tuple-element.138), channel_id=1, source_target_pairs={{0,1},{1,2},{2,3},{3,4},{4,5},{5,6},{6,7},{7,8},{8,9},{9,10},{10,1... | collective-permute-start | bytes 30728 | tf_op jit(solution)/shard_map/ppermute | solution.py:26
  131.8 31.3 %collective-permute-start.19 = (f32[132,2]{1,0:T(8,128)S(1)}, f32[132,2]{1,0:T(8,128)S(1)}, u32[]{:S(2)}, u32[]{:S(2)}) collective-permute-start(f32[132,2]{1,0:T(8,128)S(1)} %get-tuple-element.89), channel_id=1, source_target_pairs={{1,0},{2,1},{3,2},{4,3},{5,4},{6,5},{7,6},{8,7},{9,8},{10,9},{11,1... | collective-permute-start | bytes 3176 | tf_op jit(solution)/shard_map/ppermute | solution.py:28
  133.7 31.6 %collective-permute-start.18 = (f32[132,2]{1,0:T(8,128)S(1)}, f32[132,2]{1,0:T(8,128)S(1)}, u32[]{:S(2)}, u32[]{:S(2)}) collective-permute-start(f32[132,2]{1,0:T(8,128)S(1)} %get-tuple-element.88), channel_id=1, source_target_pairs={{0,1},{1,2},{2,3},{3,4},{4,5},{5,6},{6,7},{7,8},{8,9},{9,10},{10,1... | collective-permute-start | bytes 3176 | tf_op jit(solution)/shard_map/ppermute | solution.py:26
  163.1 3.1 collective-permute-start.2
  244.5 52.6 %collective-permute-start.9 = (f32[2,1,8,128]{3,2,1,0:T(8,128)S(1)}, f32[2,1,8,128]{3,2,1,0:T(8,128)S(1)}, u32[]{:S(2)}, u32[]{:S(2)}) collective-permute-start(f32[2,1,8,128]{3,2,1,0:T(8,128)S(1)} %get-tuple-element.157), channel_id=1, source_target_pairs={{16,0},{32,16},{48,32},{64,48},{80,64},{96,80},{112,96},{17,1},{33... | collective-permute-start | bytes 24584 | tf_op jit(solution)/shard_map/ppermute | solution.py:28
  250.0 47.1 %collective-permute-start.8 = (f32[2,1,8,128]{3,2,1,0:T(8,128)S(1)}, f32[2,1,8,128]{3,2,1,0:T(8,128)S(1)}, u32[]{:S(2)}, u32[]{:S(2)}) collective-permute-start(f32[2,1,8,128]{3,2,1,0:T(8,128)S(1)} %get-tuple-element.156), channel_id=1, source_target_pairs={{0,16},{16,32},{32,48},{48,64},{64,80},{80,96},{96,112},{1,17},{17... | collective-permute-start | bytes 24584 | tf_op jit(solution)/shard_map/ppermute | solution.py:26
  297.1 41.2 %collective-permute-start.11 = (f32[2,10,1,128]{3,2,1,0:T(1,128)S(1)}, f32[2,10,1,128]{3,2,1,0:T(1,128)S(1)}, u32[]{:S(2)}, u32[]{:S(2)}) collective-permute-start(f32[2,10,1,128]{3,2,1,0:T(1,128)S(1)} %get-tuple-element.134), channel_id=1, source_target_pairs={{1,0},{2,1},{3,2},{4,3},{5,4},{6,5},{7,6},{8,7},{9,8},{10,9},{11,1... | collective-permute-start | bytes 30728 | tf_op jit(solution)/shard_map/ppermute | solution.py:28
  310.1 28.3 %collective-permute-start.10 = (f32[2,10,1,128]{3,2,1,0:T(1,128)S(1)}, f32[2,10,1,128]{3,2,1,0:T(1,128)S(1)}, u32[]{:S(2)}, u32[]{:S(2)}) collective-permute-start(f32[2,10,1,128]{3,2,1,0:T(1,128)S(1)} %get-tuple-element.135), channel_id=1, source_target_pairs={{0,1},{1,2},{2,3},{3,4},{4,5},{5,6},{6,7},{7,8},{8,9},{9,10},{10,1... | collective-permute-start | bytes 30728 | tf_op jit(solution)/shard_map/ppermute | solution.py:26
  (5 other events, 12.6 us)
